TPU v7x, 256 devices: a whole 4x4x8 slice. The times are simulated.
256 devices in a mesh: ctx: 16 (over y, x), tp: 8 (over z), dp: 2 (over core).
Axes of the slice: x: 4, y: 4, z: 8, core: 2. Of those that a mesh axis runs over, the one named last changes fastest.
Arguments:
- query_latent: bfloat16 [2, 2048, 32768], P('dp', 'ctx', 'tp'), may hold values from -120 to 120
- query_rotary: bfloat16 [2, 2048, 4096], P('dp', 'ctx', 'tp'), may hold values from -6 to 6
- key_latent: bfloat16 [2, 2048, 512], P('dp', 'ctx'), may hold values from -6 to 6
- key_rotary: bfloat16 [2, 2048, 64], P('dp', 'ctx'), may hold values from -6 to 6
- value_up: bfloat16 [64, 512, 128], P('tp', 'ctx'), may hold values from -0.25 to 0.25
- out_proj: bfloat16 [64, 128, 3584], P('tp', None, 'ctx'), may hold values from -0.0625 to 0.0625
- residual: bfloat16 [2, 2048, 3584], P('dp', ('ctx', 'tp')), may hold values from -0.59765625 to 0.59765625
- norm_gain: float32 [3584], replicated, may hold values from 0.1 to 1.9
- gate_proj: bfloat16 [128, 3584, 1024], P(('ctx', 'tp'), 'dp'), may hold values from -0.09375 to 0.09375
- up_proj: bfloat16 [128, 3584, 1024], P(('ctx', 'tp'), 'dp'), may hold values from -0.09375 to 0.09375
- down_proj: bfloat16 [128, 1024, 3584], P(('ctx', 'tp'), 'dp'), may hold values from -0.1875 to 0.1875
- expert_ids: int32 [2, 2048, 8], P('dp', ('ctx', 'tp')), may hold values from 0 to 127, all different within a row; in each aligned block of 16 rows (0 to 15, 16 to 31, ..., all dimensions but the last counted through in order) at most 2 rows name the same one
- route_score: float32 [2, 2048, 8], P('dp', ('ctx', 'tp')), may hold values from 0.05 to 1
- out_grad: bfloat16 [2, 2048, 3584], P('dp', ('ctx', 'tp')), may hold values from -6 to 6
Outputs:
- layer_out: bfloat16 [2, 2048, 3584], P('dp', ('ctx', 'tp'))
- resid_grad: bfloat16 [2, 2048, 3584], P('dp', ('ctx', 'tp'))
- score_grad: float32 [2, 2048, 8], P('dp', ('ctx', 'tp'))
Inputs may be any that keep to these rules, and one draw needn't show every extreme that they name: `expert_ids`: each token names 8 different experts. In each aligned block of 16 tokens of one sequence no expert is named by more than 2 tokens, a bound that some block reaches.
All inputs are finite; a program needn't handle non-finite values.
Results may differ from a plain program's by a relative error of at most 0.034.
Values may be sent and summed in bfloat16 or wider, within the bound.
A program may use at most 128 MiB of HBM per device.

v0:
```python
import jax
import jax.numpy as jnp
from jax import lax
from jax.sharding import PartitionSpec as P

route_scale = 2.5
norm_eps = 1e-06


def rms_scale(rows_in, norm_gain):
    inverse = lax.rsqrt(jnp.mean(rows_in * rows_in, axis=-1, keepdims=True) + norm_eps)
    return rows_in * inverse * norm_gain


def expert_pass(rows_u, rows_g, gate_w, up_w, down_w):
    act_a = jnp.dot(rows_u, gate_w, preferred_element_type=jnp.float32)
    act_b = jnp.dot(rows_u, up_w, preferred_element_type=jnp.float32)
    gated_act = jax.nn.silu(act_a)
    hidden = (gated_act * act_b).astype(jnp.bfloat16)
    result = jnp.dot(hidden, down_w, preferred_element_type=jnp.float32).astype(jnp.bfloat16)
    d_hidden = jnp.dot(rows_g, down_w.T, preferred_element_type=jnp.float32)
    sigmoid_a = jax.nn.sigmoid(act_a)
    slope_a = sigmoid_a * (1.0 + act_a * (1.0 - sigmoid_a))
    d_gate = (d_hidden * act_b * slope_a).astype(jnp.bfloat16)
    d_up = (d_hidden * gated_act).astype(jnp.bfloat16)
    d_rows = jnp.dot(d_gate, gate_w.T, preferred_element_type=jnp.float32) + jnp.dot(
        d_up, up_w.T, preferred_element_type=jnp.float32
    )
    return (result, d_rows.astype(jnp.bfloat16))


def head_outputs(latent_out, value_maps):
    rows_here, head_count = (latent_out.shape[1], latent_out.shape[0])
    mapped = jnp.einsum("hqc,hcv->qhv", latent_out, value_maps, preferred_element_type=jnp.float32)
    return mapped.astype(jnp.bfloat16).reshape(rows_here, head_count * value_maps.shape[2])


def per_device(
    query_latent,
    query_rotary,
    key_latent,
    key_rotary,
    value_up,
    out_proj,
    residual,
    norm_gain,
    gate_proj,
    up_proj,
    down_proj,
    expert_ids,
    route_score,
    out_grad,
):
    ctx_count = lax.axis_size("ctx")
    tp_count = lax.axis_size("tp")
    ctx_index = lax.axis_index("ctx")
    rows_here = query_latent.shape[1]
    head_count = value_up.shape[0]
    latent_width = key_latent.shape[2]
    rope_width = key_rotary.shape[2]
    value_width = value_up.shape[2]
    model_width = residual.shape[2]
    scale = (value_width + rope_width) ** (-0.5)
    queries = query_latent[0].reshape(rows_here, head_count, latent_width)
    rotary = query_rotary[0].reshape(rows_here, head_count, rope_width)
    query_pos = ctx_index * rows_here + jnp.arange(rows_here, dtype=jnp.int32)
    last_query = ctx_index * rows_here + rows_here - 1
    initial = (
        jnp.full((head_count, rows_here), -1e30, jnp.float32),
        jnp.zeros((head_count, rows_here), jnp.float32),
        jnp.zeros((head_count, rows_here, latent_width), jnp.float32),
    )
    pieces = (
        lax.all_gather(key_latent, "ctx", axis=1, tiled=True),
        lax.all_gather(key_rotary, "ctx", axis=1, tiled=True),
    )

    def compute(running):
        row_top, row_total, weighted = running
        key_block = pieces[0][0]
        rot_block = pieces[1][0]
        key_count = key_block.shape[0]
        scores = jnp.einsum("qhc,kc->hqk", queries, key_block, preferred_element_type=jnp.float32)
        scores = scores + jnp.einsum(
            "qhr,kr->hqk", rotary, rot_block, preferred_element_type=jnp.float32
        )
        key_pos = jnp.arange(key_count, dtype=jnp.int32)
        causal = key_pos[None, None, :] <= query_pos[None, :, None]
        scores = jnp.where(causal, scores * scale, -1e30)
        new_top = jnp.maximum(row_top, jnp.max(scores, axis=2))
        exp_terms = jnp.where(causal, jnp.exp(scores - new_top[:, :, None]), 0.0)
        row_total = jnp.sum(exp_terms, axis=2)
        weighted = jnp.einsum(
            "hqk,kc->hqc",
            exp_terms.astype(jnp.bfloat16),
            key_block,
            preferred_element_type=jnp.float32,
        )
        return (new_top, row_total, weighted)

    row_top, row_total, weighted = lax.cond(
        jnp.int32(0) <= last_query, compute, lambda running: running, initial
    )
    latent_out = (weighted / row_total[:, :, None]).astype(jnp.bfloat16)
    tok_rows = rows_here // tp_count
    value_maps, out_maps = (
        lax.all_gather(value_up, "ctx", axis=1, tiled=True),
        lax.all_gather(out_proj, "ctx", axis=2, tiled=True),
    )
    heads_out = head_outputs(latent_out, value_maps)
    flat_out = out_maps.reshape(head_count * value_width, model_width)
    attn_rows = lax.psum_scatter(
        jnp.dot(heads_out, flat_out, preferred_element_type=jnp.float32).astype(jnp.bfloat16),
        "tp",
        scatter_dimension=0,
        tiled=True,
    ).astype(jnp.float32)
    hidden_sum = residual[0].astype(jnp.float32) + attn_rows
    normed = rms_scale(hidden_sum, norm_gain).astype(jnp.bfloat16)
    route_ids = expert_ids[0]
    top_count = route_ids.shape[1]
    experts = ctx_count * tp_count
    capacity = 2 * tok_rows * top_count // experts
    flat_ids = route_ids.reshape(tok_rows * top_count)
    chosen = (flat_ids[:, None] == jnp.arange(experts, dtype=jnp.int32)[None, :]).astype(jnp.int32)
    earlier = jnp.cumsum(chosen, axis=0) - chosen
    slot_index = jnp.sum(earlier * chosen, axis=1)
    target = flat_ids * capacity + slot_index
    select = (target[:, None] == jnp.arange(experts * capacity, dtype=jnp.int32)[None, :]).astype(
        jnp.bfloat16
    )
    placing = jnp.sum(select.reshape(tok_rows, top_count, experts * capacity), axis=1)
    paired = jnp.concatenate([normed, out_grad[0]], axis=1)
    outgoing = jnp.dot(placing.T, paired, preferred_element_type=jnp.float32).astype(jnp.bfloat16)
    outgoing = outgoing.reshape(experts, capacity, 2, model_width)
    gate_full, up_full, down_full = (
        lax.all_gather(gate_proj, "dp", axis=1, tiled=True),
        lax.all_gather(up_proj, "dp", axis=1, tiled=True),
        lax.all_gather(down_proj, "dp", axis=1, tiled=True),
    )
    gate_w = gate_full[0]
    up_w = up_full[0]
    down_w = down_full[0]
    arrived = lax.all_to_all(outgoing, ("ctx", "tp"), split_axis=0, concat_axis=0, tiled=True)
    sources = arrived.shape[0]
    slot_count = arrived.shape[1]
    slot_rows = arrived.reshape(sources * slot_count, 2, model_width)
    result, d_rows = expert_pass(slot_rows[:, 0], slot_rows[:, 1], gate_w, up_w, down_w)
    going_back = jnp.stack([result, d_rows], axis=1).reshape(sources, slot_count, 2, model_width)
    returned = lax.all_to_all(going_back, ("ctx", "tp"), split_axis=0, concat_axis=0, tiled=True)
    per_route = jnp.dot(
        select,
        returned.reshape(experts * capacity, 2 * model_width),
        preferred_element_type=jnp.float32,
    )
    per_route = per_route.reshape(tok_rows, top_count, 2, model_width)
    route_out = per_route[:, :, 0]
    route_grad = per_route[:, :, 1]
    route_raw = route_score[0]
    score_total = jnp.sum(route_raw, axis=1, keepdims=True)
    route_weight = route_scale * route_raw / score_total
    mixed_out = hidden_sum + jnp.einsum(
        "tk,tkd->td", route_weight, route_out, precision=lax.Precision.HIGHEST
    )
    grad_rows = out_grad[0].astype(jnp.float32)
    weight_grad = jnp.einsum("td,tkd->tk", grad_rows, route_out, precision=lax.Precision.HIGHEST)
    d_normed = jnp.einsum("tk,tkd->td", route_weight, route_grad, precision=lax.Precision.HIGHEST)
    unused, pullback = jax.vjp(lambda rows_in: rms_scale(rows_in, norm_gain), hidden_sum)
    resid_grad = (grad_rows + pullback(d_normed)[0]).astype(jnp.bfloat16)
    score_grad = (
        route_scale
        / score_total
        * (weight_grad - jnp.sum(weight_grad * route_raw, axis=1, keepdims=True) / score_total)
    )
    return (mixed_out.astype(jnp.bfloat16)[None], resid_grad[None], score_grad[None])


def solution(mesh):
    return jax.shard_map(
        per_device,
        mesh=mesh,
        in_specs=(
            P("dp", "ctx", "tp"),
            P("dp", "ctx", "tp"),
            P("dp", "ctx", None),
            P("dp", "ctx", None),
            P("tp", "ctx", None),
            P("tp", None, "ctx"),
            P("dp", ("ctx", "tp"), None),
            P(),
            P(("ctx", "tp"), "dp", None),
            P(("ctx", "tp"), "dp", None),
            P(("ctx", "tp"), "dp", None),
            P("dp", ("ctx", "tp"), None),
            P("dp", ("ctx", "tp"), None),
            P("dp", ("ctx", "tp"), None),
        ),
        out_specs=(
            P("dp", ("ctx", "tp"), None),
            P("dp", ("ctx", "tp"), None),
            P("dp", ("ctx", "tp"), None),
        ),
        check_vma=False,
    )
```

profile of v0, /device:TPU:32, one launch (start us, length us, event | category | flops | bytes accessed | tf_op | source)
XLA Modules:
  0.0 521.7 jit_solution(13411717028966328108)
XLA Ops:
  8.0 0.7 all-gather.7.cloned.1.call-update
  8.7 0.0 all-gather.9.cloned.1.call-start
  8.8 0.7 all-gather.9.cloned.1.call-update
  9.5 0.7 all-gather.11.cloned.1.call-update
  10.2 0.0 reduce-scatter.2.cloned.1.call-start
  10.3 24.5 %all_gather.22 = bf16[1,2048,64]{1,2,0:T(8,128)(2,1)S(1)} all-gather(bf16[1,128,64]{1,2,0:T(8,128)(2,1)} %param.19), channel_id=1, replica_groups=mesh['ctx'=16,'tp'=8,'dp'=2] {'ctx'}, dimensions={1}, use_global_device_ids=true | all-gather | bytes 278528 | tf_op jit(solution)/shard_map/all_gather | solution.py:75
  34.7 29.1 %all-gather.7.cloned.1.call-done = bf16[1,2048,512]{2,1,0:T(8,128)(2,1)} async-done(((bf16[1,128,512]{2,1,0:T(8,128)(2,1)}), bf16[1,2048,512]{2,1,0:T(8,128)(2,1)}) %all-gather.7.cloned.1.call-update) | async-done | bytes 2097168 | tf_op jit(solution)/shard_map/all_gather | solution.py:74
  63.8 17.5 %conditional.1 = (f32[8,128]{1,0:T(8,128)S(1)}, f32[8,128,512]{2,1,0:T(8,128)S(1)}) conditional(s32[]{:T(128)} %convert_element_type.68, () %tuple.16, (s32[]{:T(128)}, s32[128]{0:T(128)S(1)}, bf16[1,2048,512]{2,1,0:T(8,128)(2,1)}, bf16[1,128,4096]{2,1,0:T(8,128)(2,1)}, bf16[1,2048,64]{1,2,0:T(8,128)(2,1)S(1)}, ...), branch_computations={%region_0.0_spmd, %region_1.4_spmd} | conditional | flops 4584635392 | bytes 62023244 | solution.py:101
  63.9 0.2 iota_compare_fusion
  64.0 1.6 copy.58
  65.7 6.4 %fusion.8 = f32[2048,128,8]{1,0,2:T(8,128)} fusion(bf16[1,2048,512]{2,1,0:T(8,128)(2,1)} %get-tuple-element.18, bf16[128,8,512]{2,1,0:T(8,128)(2,1)S(1)} %bitcast.136), kind=kOutput, calls=%fused_computation.9 | convolution fusion | flops 2147483648 | bytes 11534336 | tf_op jit(solution)/shard_map/cond/branch_1_fun/qhc,kc->hqk/dot_general | solution.py:83
  72.1 0.1 copy.39
  72.2 5.2 fusion.69
  77.4 2.4 fusion.2
  79.9 1.4 fusion.1
  81.3 32.7 %all-gather.9.cloned.1.call-done = bf16[8,512,128]{2,1,0:T(8,128)(2,1)} async-done(((bf16[8,32,128]{2,1,0:T(8,128)(2,1)}), bf16[8,512,128]{2,1,0:T(8,128)(2,1)}) %all-gather.9.cloned.1.call-update) | async-done | bytes 1048592 | tf_op jit(solution)/shard_map/all_gather | solution.py:107
  114.0 73.1 %all-gather.11.cloned.1.call-done = bf16[8,128,3584]{1,2,0:T(8,128)(2,1)} async-done(((bf16[8,128,224]{1,2,0:T(8,128)(2,1)}), bf16[8,128,3584]{1,2,0:T(8,128)(2,1)}) %all-gather.11.cloned.1.call-update) | async-done | bytes 7340048 | tf_op jit(solution)/shard_map/all_gather | solution.py:108
  187.1 7.2 %fusion.34 = bf16[128,3584]{1,0:T(8,128)(2,1)} fusion(bf16[8,128,3584]{1,2,0:T(8,128)(2,1)} %all-gather.11.cloned.1.call-done, bf16[8,512,128]{2,1,0:T(8,128)(2,1)} %all-gather.9.cloned.1.call-done, f32[8,128,512]{2,1,0:T(8,128)S(1)} %get-tuple-element.27, f32[8,128]{1,0:T(8,128)S(1)} %get-tuple-element.28), kind=kOutput, calls=%fused_computation.34 | convolution fusion | flops 1075380224 | bytes 11407360 | tf_op jit(solution)/shard_map/dot_general | solution.py:113
  194.4 0.0 all-gather.13.cloned.1.call-start
  194.5 0.5 all-gather.13.cloned.1.call-update
  195.0 11.6 %all-gather.15.cloned.1.call-start = ((), (), s32[]{:S(2)}) async-start(), calls=%async_computation.8 | async-start | bytes 11010048 | tf_op jit(solution)/shard_map/all_gather | solution.py:138
  206.6 0.1 copy.40
  206.7 0.1 eq.51
  206.8 0.1 fusion.58
  206.9 0.2 reduce_window_sum.11
  207.1 0.2 select_reduce_fusion
  207.3 0.1 reduce_sum.78
  207.3 0.1 copy.41
  207.4 0.1 copy.42
  207.5 0.1 fusion.56
  207.6 24.1 %reduce-scatter.2.cloned.1.call-done = bf16[16,3584]{1,0:T(8,128)(2,1)} async-done(((bf16[128,3584]{1,0:T(8,128)(2,1)}), bf16[16,3584]{1,0:T(8,128)(2,1)}) %reduce-scatter.2.cloned.1.call-update) | async-done | bytes 114704 | tf_op jit(solution)/shard_map/reduce_scatter | solution.py:112
  231.7 1.0 multiply_reduce_fusion.1
  232.8 1.0 multiply_convert_fusion.6
  233.8 3.0 convolution_convert_fusion
  236.8 9.5 %reshape.124 = bf16[128,2,2,3584]{3,2,1,0:T(2,128)(2,1)} reshape(bf16[256,7168]{1,0:T(8,128)(2,1)} %convolution_convert_fusion) | data formatting | bytes 7340032 | tf_op jit(solution)/shard_map/reshape | solution.py:135
  246.3 12.2 %all-to-all-start = ((bf16[128,2,2,3584]{3,2,1,0:T(2,128)(2,1)}), bf16[128,2,2,3584]{3,2,1,0:T(2,128)(2,1)}, u32[]{:S(2)}, u32[]{:S(2)}) async-start(bf16[128,2,2,3584]{3,2,1,0:T(2,128)(2,1)} %reshape.124), calls=%async_computation.1 | async-start | bytes 7340032 | tf_op jit(solution)/shard_map/all_to_all | solution.py:144
  258.4 0.0 all-gather.17.cloned.1.call-start
  258.5 0.5 all-gather.17.cloned.1.call-update
  259.0 82.3 %all-to-all-done = bf16[128,2,2,3584]{3,2,1,0:T(2,128)(2,1)} async-done(((bf16[128,2,2,3584]{3,2,1,0:T(2,128)(2,1)}), bf16[128,2,2,3584]{3,2,1,0:T(2,128)(2,1)}, u32[]{:S(2)}, u32[]{:S(2)}) %all-to-all-start) | async-done | bytes 3670048 | tf_op jit(solution)/shard_map/all_to_all | solution.py:144
  341.3 8.9 %fusion.70 = (bf16[256,1,3584]{2,1,0:T(2,128)(2,1)}, bf16[256,1,3584]{2,1,0:T(2,128)(2,1)}) fusion(bf16[256,2,3584]{2,1,0:T(2,128)(2,1)} %bitcast.16), kind=kLoop, calls=%fused_computation.96 | loop fusion | bytes 7340032 | tf_op jit(solution)/shard_map/slice | solution.py:148
  350.2 6.3 %fusion.23 = f32[256,1024]{1,0:T(8,128)S(1)} fusion(bf16[1,3584,1024]{2,1,0:T(8,128)(2,1)} %all-gather.13.cloned.1.call-done, bf16[256,1,3584]{2,1,0:T(2,128)(2,1)} %get-tuple-element.53), kind=kOutput, calls=%fused_computation.28 | convolution fusion | flops 1879048192 | bytes 10223616 | tf_op jit(solution)/shard_map/dot_general | solution.py:16
  356.5 7.3 %fusion.19 = f32[256,1024]{1,0:T(8,128)} fusion(bf16[1,3584,1024]{2,1,0:T(8,128)(2,1)} %all-gather.15.cloned.1.call-done, bf16[256,1,3584]{2,1,0:T(2,128)(2,1)} %get-tuple-element.53), kind=kOutput, calls=%fused_computation.24 | convolution fusion | flops 1879048192 | bytes 10223616 | tf_op jit(solution)/shard_map/dot_general | solution.py:17
  363.8 6.4 %fusion.13 = f32[256,1024]{1,0:T(8,128)S(1)} fusion(bf16[1,1024,3584]{2,1,0:T(8,128)(2,1)} %all-gather.17.cloned.1.call-done, bf16[256,1,3584]{2,1,0:T(2,128)(2,1)} %get-tuple-element.54), kind=kOutput, calls=%fused_computation.18 | convolution fusion | flops 1879048192 | bytes 10223616 | tf_op jit(solution)/shard_map/dot_general | solution.py:21
  370.2 1.0 copy-done.10
  371.2 2.2 fusion.17
  373.4 3.9 fusion.31
  377.3 3.7 stack.13
  381.0 5.5 %fusion.28 = bf16[256,3584]{1,0:T(8,128)(2,1)S(1)} fusion(bf16[1,1024,3584]{2,1,0:T(8,128)(2,1)} %all-gather.17.cloned.1.call-done, f32[256,1024]{1,0:T(8,128)} %fusion.19, f32[256,1024]{1,0:T(8,128)S(1)} %fusion.23), kind=kOutput, calls=%fused_computation.31 | convolution fusion | flops 1881538560 | bytes 11272192 | tf_op jit(solution)/shard_map/dot_general | solution.py:20
  386.5 3.8 stack.12
  390.3 9.8 %pad_maximum_fusion = bf16[128,2,2,3584]{3,2,1,0:T(2,128)(2,1)} fusion(bf16[128,2,1,3584]{3,2,1,0:T(2,128)(2,1)} %stack.13, bf16[128,2,1,3584]{3,2,1,0:T(2,128)(2,1)} %stack.12), kind=kLoop, calls=%fused_computation.35 | loop fusion | flops 7340032 | bytes 7340032 | tf_op jit(solution)/shard_map/stack | solution.py:149
  400.1 7.8 %all-to-all-start.1 = ((bf16[128,2,2,3584]{3,2,1,0:T(2,128)(2,1)}), bf16[128,2,2,3584]{3,2,1,0:T(2,128)(2,1)}, u32[]{:S(2)}, u32[]{:S(2)}) async-start(bf16[128,2,2,3584]{3,2,1,0:T(2,128)(2,1)} %pad_maximum_fusion), calls=%async_computation.2 | async-start | bytes 7340032 | tf_op jit(solution)/shard_map/all_to_all | solution.py:150
  408.0 80.6 %all-to-all-done.1 = bf16[128,2,2,3584]{3,2,1,0:T(2,128)(2,1)} async-done(((bf16[128,2,2,3584]{3,2,1,0:T(2,128)(2,1)}), bf16[128,2,2,3584]{3,2,1,0:T(2,128)(2,1)}, u32[]{:S(2)}, u32[]{:S(2)}) %all-to-all-start.1) | async-done | bytes 3670048 | tf_op jit(solution)/shard_map/all_to_all | solution.py:150
  488.6 4.4 copy.59
  493.0 5.9 %copy.47 = bf16[7168,256]{1,0:T(8,128)(2,1)} copy(bf16[7168,256]{0,1:T(8,128)(2,1)} %bitcast.133) | data formatting | bytes 7340032 | tf_op jit(solution)/shard_map/dot_general | solution.py:151
  499.0 3.4 fusion.51
  502.4 1.8 copy-done
  504.1 1.9 fusion.36
  506.1 0.1 copy.54
  506.2 0.1 copy.50
  506.2 3.1 fusion.37
  509.3 3.1 fusion.35
  512.5 0.2 multiply_reduce_fusion
  512.6 0.6 fusion.61
  513.2 0.8 fusion.55
  (41 shorter events, 0.3 us)
Async XLA Ops:
  8.0 55.8 %all-gather.7.cloned.1.call-start = ((), (), s32[]{:S(2)}) async-start(), calls=%async_computation.3 | async-start | bytes 2228224 | tf_op jit(solution)/shard_map/all_gather | solution.py:74
  8.7 105.3 %all-gather.9.cloned.1.call-start = ((), (), s32[]{:S(2)}) async-start(), calls=%async_computation.4 | async-start | bytes 1114112 | tf_op jit(solution)/shard_map/all_gather | solution.py:107
  9.5 177.6 %all-gather.11.cloned.1.call-start = ((), (), s32[]{:S(2)}) async-start(), calls=%async_computation.5 | async-start | bytes 7798784 | tf_op jit(solution)/shard_map/all_gather | solution.py:108
  10.2 221.5 %reduce-scatter.2.cloned.1.call-start = ((), (), s32[]{:S(2)}) async-start(), calls=%async_computation.6 | async-start | bytes 1032192 | tf_op jit(solution)/shard_map/reduce_scatter | solution.py:112
  65.7 6.4 %copy-start.5 = (bf16[1,128,512]{2,1,0:T(8,128)(2,1)S(1)}, bf16[1,128,512]{2,1,0:T(8,128)(2,1)}, u32[]{:S(2)}) copy-start(bf16[1,128,512]{2,1,0:T(8,128)(2,1)} %get-tuple-element.50) | copy-start | bytes 393220 | tf_op jit(solution)/shard_map/cond
  72.2 5.2 %copy-start.9 = (bf16[1,2048,512]{2,1,0:T(8,128)(2,1)S(1)}, bf16[1,2048,512]{2,1,0:T(8,128)(2,1)}, u32[]{:S(2)}) copy-start(bf16[1,2048,512]{2,1,0:T(8,128)(2,1)} %get-tuple-element.18) | copy-start | bytes 6291460 | tf_op jit(solution)/shard_map/cond
  194.4 12.3 %copy-start.6 = (s32[1,16,8]{1,2,0:T(8,128)S(1)}, s32[1,16,8]{1,2,0:T(8,128)}, u32[]{:S(2)}) copy-start(s32[1,16,8]{1,2,0:T(8,128)} %param.27) | copy-start | bytes 1540
  194.4 37.4 %copy-start.1 = (bf16[1,16,3584]{2,1,0:T(8,128)(2,1)S(1)}, bf16[1,16,3584]{2,1,0:T(8,128)(2,1)}, u32[]{:S(2)}) copy-start(bf16[1,16,3584]{2,1,0:T(8,128)(2,1)} %param.22) | copy-start | bytes 344068
  194.4 38.4 %copy-start.4 = (f32[3584]{0:T(1024)S(1)}, f32[3584]{0:T(1024)}, u32[]{:S(2)}) copy-start(f32[3584]{0:T(1024)} %param.23) | copy-start | bytes 43012
  194.4 39.4 %copy-start.3 = (bf16[1,16,3584]{2,1,0:T(8,128)(2,1)S(1)}, bf16[1,16,3584]{2,1,0:T(8,128)(2,1)}, u32[]{:S(2)}) copy-start(bf16[1,16,3584]{2,1,0:T(8,128)(2,1)} %param.29) | copy-start | bytes 344068
  194.4 155.8 %all-gather.13.cloned.1.call-start = ((), (), s32[]{:S(2)}) async-start(), calls=%async_computation.7 | async-start | bytes 11010048 | tf_op jit(solution)/shard_map/all_gather | solution.py:137
  195.0 161.5 %all-gather.15.cloned.1.call-start = ((), (), s32[]{:S(2)}) async-start(), calls=%async_computation.8 | async-start | bytes 11010048 | tf_op jit(solution)/shard_map/all_gather | solution.py:138
  246.3 95.0 %all-to-all-start = ((bf16[128,2,2,3584]{3,2,1,0:T(2,128)(2,1)}), bf16[128,2,2,3584]{3,2,1,0:T(2,128)(2,1)}, u32[]{:S(2)}, u32[]{:S(2)}) async-start(bf16[128,2,2,3584]{3,2,1,0:T(2,128)(2,1)} %reshape.124), calls=%async_computation.1 | async-start | bytes 7340032 | tf_op jit(solution)/shard_map/all_to_all | solution.py:144
  258.4 105.3 %all-gather.17.cloned.1.call-start = ((), (), s32[]{:S(2)}) async-start(), calls=%async_computation.9 | async-start | bytes 11010048 | tf_op jit(solution)/shard_map/all_gather | solution.py:139
  363.8 7.4 %copy-start.8 = (bf16[1,3584,1024]{2,1,0:T(8,128)(2,1)S(1)}, bf16[1,3584,1024]{2,1,0:T(8,128)(2,1)}, u32[]{:S(2)}) copy-start(bf16[1,3584,1024]{2,1,0:T(8,128)(2,1)} %all-gather.15.cloned.1.call-done) | copy-start | bytes 22020100
  363.8 9.6 %slice-start = ((s8[7340032]{0:T(1024)(128)(4,1)}), s8[4194304]{0:T(1024)(128)(4,1)S(1)}, s32[]{:S(2)}) async-start(s8[7340032]{0:T(1024)(128)(4,1)} %bitcast.140), calls=%async_computation.10 | async-start | bytes 8388608
  370.2 1.0 copy-start.10
  371.2 2.2 slice-start.1
  400.1 7.8 %copy-start.7 = (f32[1,16,8]{1,2,0:T(8,128)S(1)}, f32[1,16,8]{1,2,0:T(8,128)}, u32[]{:S(2)}) copy-start(f32[1,16,8]{1,2,0:T(8,128)} %param.28) | copy-start | bytes 1540
  400.1 88.5 %all-to-all-start.1 = ((bf16[128,2,2,3584]{3,2,1,0:T(2,128)(2,1)}), bf16[128,2,2,3584]{3,2,1,0:T(2,128)(2,1)}, u32[]{:S(2)}, u32[]{:S(2)}) async-start(bf16[128,2,2,3584]{3,2,1,0:T(2,128)(2,1)} %pad_maximum_fusion), calls=%async_computation.2 | async-start | bytes 7340032 | tf_op jit(solution)/shard_map/all_to_all | solution.py:150
  502.3 1.8 copy-start
  502.3 10.1 %copy-start.2 = (bf16[16,3584]{1,0:T(8,128)(2,1)S(1)}, bf16[16,3584]{1,0:T(8,128)(2,1)}, u32[]{:S(2)}) copy-start(bf16[16,3584]{1,0:T(8,128)(2,1)} %reduce-scatter.2.cloned.1.call-done) | copy-start | bytes 344068
Sparse Core Ops, SparseCore 0:
  11.3 52.5 all-gather.6
  66.2 47.7 all-gather.8
  116.5 70.5 all-gather.10
  194.5 37.1 reduce-scatter.1
Sparse Core Ops, SparseCore 1:
  196.8 23.3 all-gather.12
  221.9 24.8 all-gather.14
  260.8 24.9 all-gather.16
where the time goes:
time: 530 us; the launch traced here: 522 us
  waiting for transfers between devices  325 us (61%)
  matrix products  67.2 us (13%)
  local copies, waits for them, and re-layouts  41.3 us (8%)
  starting transfers between devices  31.9 us (6%)
  blocking collectives  24.5 us (5%)
  between operations  16.1 us (3%)
  other arithmetic  15.6 us (3%)
    all_to_all x1, waiting for transfers between devices, per_device(): lax.all_to_all(outgoing, ('ctx', 'tp'), split_axis=0, concat_axis=0, tile...  82.3 us
    all_to_all x1, waiting for transfers between devices, per_device(): lax.all_to_all(going_back, ('ctx', 'tp'), split_axis=0, concat_axis=0, ti...  80.6 us
    all_gather x1, waiting for transfers between devices, per_device(): lax.all_gather(out_proj, 'ctx', axis=2, tiled=True)  73.1 us
    all_gather x1, waiting for transfers between devices, per_device(): lax.all_gather(value_up, 'ctx', axis=1, tiled=True)  32.7 us
    all_gather x1, waiting for transfers between devices, per_device(): lax.all_gather(key_latent, 'ctx', axis=1, tiled=True)  29.1 us
    all_gather x1, blocking collectives, per_device(): lax.all_gather(key_rotary, 'ctx', axis=1, tiled=True)  24.5 us
    reduce_scatter x1, waiting for transfers between devices, per_device(): lax.psum_scatter(jnp.dot(heads_out, flat_out, preferred_element_type=jnp....  24.1 us
    all_to_all x1, starting transfers between devices, per_device(): lax.all_to_all(outgoing, ('ctx', 'tp'), split_axis=0, concat_axis=0, tile...  12.2 us
  transfers between devices with their start and end apart: 9, of which 6 were waited for; matrix products, arithmetic and copies ran while one was open for 11% of the time, Pallas kernels for 0%

commit v1 on v0

--- a/solution.py
+++ b/solution.py
@@ -105,7 +105,9 @@
     tok_rows = rows_here // tp_count
     value_maps, out_maps = (
         lax.all_gather(value_up, "ctx", axis=1, tiled=True),
-        lax.all_gather(out_proj, "ctx", axis=2, tiled=True),
+        jnp.concatenate(
+            lax.all_to_all(jnp.stack([out_proj] * lax.axis_size("ctx")), "ctx", 0, 0), axis=2
+        ),
     )
     heads_out = head_outputs(latent_out, value_maps)
     flat_out = out_maps.reshape(head_count * value_width, model_width)

time: 530 us -> 538 us (1.015)
  waiting for transfers between devices: 325 us -> 212 us
  blocking collectives: 24.5 us -> 130 us
  starting transfers between devices: 31.9 us -> 38.9 us
  local copies, waits for them, and re-layouts: 41.3 us -> 46.9 us
    all_gather x1, blocking collectives: 24.5 us -> 130 us  [per_device(): lax.all_gather(key_rotary, 'ctx', axis=1, tiled=True)]
    all_gather x1 -> x0, waiting for transfers between devices: 73.1 us -> none  [per_device(): lax.all_gather(out_proj, 'ctx', axis=2, tiled=True)]
    all_gather x1, waiting for transfers between devices: 29.1 us -> 0.01 us  [per_device(): lax.all_gather(key_latent, 'ctx', axis=1, tiled=True)]
    all_gather x1, waiting for transfers between devices: 32.7 us -> 22.3 us  [per_device(): lax.all_gather(value_up, 'ctx', axis=1, tiled=True)]
    all_to_all x0 -> x1, starting transfers between devices: none -> 7.21 us  [per_device(): lax.all_to_all(jnp.stack([out_proj] * lax.axis_size('ctx')), 'ctx', 0, 0)]
  transfers between devices with their start and end apart: 9 -> 9, of which waited for: 6 -> 4; matrix products, arithmetic and copies ran while one was open for 11% -> 11% of each run, Pallas kernels for 0% -> 0%
where the time goes in v1:
time: 538 us; the launch traced here: 528 us
  waiting for transfers between devices  212 us (39%)
  blocking collectives  130 us (24%)
  matrix products  68.5 us (13%)
  local copies, waits for them, and re-layouts  46.9 us (9%)
  starting transfers between devices  38.9 us (7%)
  between operations  16.1 us (3%)
  other arithmetic  15.6 us (3%)
    all_gather x1, blocking collectives, per_device(): lax.all_gather(key_rotary, 'ctx', axis=1, tiled=True)  130 us
    all_to_all x1, waiting for transfers between devices, per_device(): lax.all_to_all(outgoing, ('ctx', 'tp'), split_axis=0, concat_axis=0, tile...  82.5 us
    all_to_all x1, waiting for transfers between devices, per_device(): lax.all_to_all(going_back, ('ctx', 'tp'), split_axis=0, concat_axis=0, ti...  81 us
    reduce_scatter x1, waiting for transfers between devices, per_device(): lax.psum_scatter(jnp.dot(heads_out, flat_out, preferred_element_type=jnp....  23.8 us
    all_gather x1, waiting for transfers between devices, per_device(): lax.all_gather(value_up, 'ctx', axis=1, tiled=True)  22.3 us
    all_to_all x1, starting transfers between devices, per_device(): lax.all_to_all(outgoing, ('ctx', 'tp'), split_axis=0, concat_axis=0, tile...  12.1 us
    all_gather x1, starting transfers between devices, per_device(): lax.all_gather(up_proj, 'dp', axis=1, tiled=True)  11.6 us
  transfers between devices with their start and end apart: 9, of which 4 were waited for; matrix products, arithmetic and copies ran while one was open for 11% of the time, Pallas kernels for 0%

profile of v1, /device:TPU:32, one launch (start us, length us, event | category | flops | bytes accessed | tf_op | source)
XLA Modules:
  0.0 527.9 jit_solution(17410858688959551954)
XLA Ops:
  8.0 1.2 copy.42
  9.2 4.4 stack.8
  13.6 7.2 %all-to-all-start = ((bf16[16,8,128,224]{2,1,3,0:T(8,128)(2,1)}), bf16[16,8,128,224]{2,1,3,0:T(8,128)(2,1)}, u32[]{:S(2)}, u32[]{:S(2)}) async-start(bf16[16,8,128,224]{2,1,3,0:T(8,128)(2,1)} %stack.8), calls=%async_computation | async-start | bytes 14680064 | tf_op jit(solution)/shard_map/all_to_all | solution.py:109
  20.8 0.0 all-gather.6.cloned.1.call-start
  20.9 0.7 all-gather.6.cloned.1.call-update
  21.6 0.7 all-gather.8.cloned.1.call-update
  22.4 129.7 %all_gather.19 = bf16[1,2048,64]{1,2,0:T(8,128)(2,1)S(1)} all-gather(bf16[1,128,64]{1,2,0:T(8,128)(2,1)S(1)} %copy-done.6), channel_id=1, replica_groups=mesh['ctx'=16,'tp'=8,'dp'=2] {'ctx'}, dimensions={1}, use_global_device_ids=true | all-gather | bytes 278528 | tf_op jit(solution)/shard_map/all_gather | solution.py:75
  152.1 17.5 %conditional.1 = (f32[8,128]{1,0:T(8,128)S(1)}, f32[8,128,512]{2,1,0:T(8,128)S(1)}) conditional(s32[]{:T(128)} %convert_element_type.68, () %tuple.16, (s32[]{:T(128)}, s32[128]{0:T(128)S(1)}, bf16[1,2048,512]{2,1,0:T(8,128)(2,1)}, bf16[1,128,4096]{2,1,0:T(8,128)(2,1)}, bf16[1,2048,64]{1,2,0:T(8,128)(2,1)S(1)}, ...), branch_computations={%region_0.0_spmd, %region_1.4_spmd} | conditional | flops 4584635392 | bytes 61498928 | solution.py:101
  152.1 0.2 iota_compare_fusion
  152.3 1.6 copy.61
  153.9 6.4 %fusion.8 = f32[2048,128,8]{1,0,2:T(8,128)} fusion(bf16[1,2048,512]{2,1,0:T(8,128)(2,1)} %get-tuple-element.18, bf16[128,8,512]{2,1,0:T(8,128)(2,1)S(1)} %bitcast.141), kind=kOutput, calls=%fused_computation.9 | convolution fusion | flops 2147483648 | bytes 11534336 | tf_op jit(solution)/shard_map/cond/branch_1_fun/qhc,kc->hqk/dot_general | solution.py:83
  160.4 0.1 copy.41
  160.5 5.2 fusion.73
  165.7 2.4 fusion.2
  168.2 1.4 fusion.1
  169.6 22.3 %all-gather.8.cloned.1.call-done = bf16[8,512,128]{2,1,0:T(8,128)(2,1)} async-done(((bf16[8,32,128]{2,1,0:T(8,128)(2,1)}), bf16[8,512,128]{2,1,0:T(8,128)(2,1)}) %all-gather.8.cloned.1.call-update) | async-done | bytes 1048592 | tf_op jit(solution)/shard_map/all_gather | solution.py:107
  191.9 1.9 convolution_convert_fusion.1
  193.8 6.6 %fusion.37 = bf16[128,3584]{1,0:T(8,128)(2,1)} fusion(bf16[128,1024]{0,1:T(8,128)(2,1)S(1)} %bitcast.147, bf16[448,8,8,128]{3,2,1,0:T(8,128)(2,1)} %bitcast.44), kind=kOutput, calls=%fused_computation.36 | convolution fusion | flops 939982848 | bytes 8519680 | tf_op jit(solution)/shard_map/dot_general | solution.py:115
  200.4 0.0 all-gather.10.cloned.1.call-start
  200.5 0.5 all-gather.10.cloned.1.call-update
  201.0 11.6 %all-gather.12.cloned.1.call-start = ((), (), s32[]{:S(2)}) async-start(), calls=%async_computation.8 | async-start | bytes 11010048 | tf_op jit(solution)/shard_map/all_gather | solution.py:140
  212.7 0.1 copy.43
  212.7 0.1 eq.51
  212.8 0.1 fusion.62
  212.9 0.2 reduce_window_sum.11
  213.1 0.2 select_reduce_fusion
  213.3 0.1 reduce_sum.78
  213.3 0.1 copy.44
  213.4 0.1 copy.45
  213.5 0.1 fusion.60
  213.6 23.8 %reduce-scatter.2.cloned.1.call-done = bf16[16,3584]{1,0:T(8,128)(2,1)} async-done(((bf16[128,3584]{1,0:T(8,128)(2,1)}), bf16[16,3584]{1,0:T(8,128)(2,1)}) %reduce-scatter.2.cloned.1.call-update) | async-done | bytes 114704 | tf_op jit(solution)/shard_map/reduce_scatter | solution.py:114
  237.5 1.0 multiply_reduce_fusion.1
  238.5 1.0 multiply_convert_fusion.6
  239.5 3.0 convolution_convert_fusion
  242.6 9.5 %reshape.132 = bf16[128,2,2,3584]{3,2,1,0:T(2,128)(2,1)} reshape(bf16[256,7168]{1,0:T(8,128)(2,1)} %convolution_convert_fusion) | data formatting | bytes 7340032 | tf_op jit(solution)/shard_map/reshape | solution.py:137
  252.0 12.1 %all-to-all-start.1 = ((bf16[128,2,2,3584]{3,2,1,0:T(2,128)(2,1)}), bf16[128,2,2,3584]{3,2,1,0:T(2,128)(2,1)}, u32[]{:S(2)}, u32[]{:S(2)}) async-start(bf16[128,2,2,3584]{3,2,1,0:T(2,128)(2,1)} %reshape.132), calls=%async_computation.2 | async-start | bytes 7340032 | tf_op jit(solution)/shard_map/all_to_all | solution.py:146
  264.1 0.0 all-gather.14.cloned.1.call-start
  264.1 0.5 all-gather.14.cloned.1.call-update
  264.7 82.5 %all-to-all-done.1 = bf16[128,2,2,3584]{3,2,1,0:T(2,128)(2,1)} async-done(((bf16[128,2,2,3584]{3,2,1,0:T(2,128)(2,1)}), bf16[128,2,2,3584]{3,2,1,0:T(2,128)(2,1)}, u32[]{:S(2)}, u32[]{:S(2)}) %all-to-all-start.1) | async-done | bytes 3670048 | tf_op jit(solution)/shard_map/all_to_all | solution.py:146
  347.2 8.9 %fusion.74 = (bf16[256,1,3584]{2,1,0:T(2,128)(2,1)}, bf16[256,1,3584]{2,1,0:T(2,128)(2,1)}) fusion(bf16[256,2,3584]{2,1,0:T(2,128)(2,1)} %bitcast.17), kind=kLoop, calls=%fused_computation.97 | loop fusion | bytes 7340032 | tf_op jit(solution)/shard_map/slice | solution.py:150
  356.1 6.3 %fusion.26 = f32[256,1024]{1,0:T(8,128)S(1)} fusion(bf16[1,3584,1024]{2,1,0:T(8,128)(2,1)} %all-gather.10.cloned.1.call-done, bf16[256,1,3584]{2,1,0:T(2,128)(2,1)} %get-tuple-element.53), kind=kOutput, calls=%fused_computation.31 | convolution fusion | flops 1879048192 | bytes 10223616 | tf_op jit(solution)/shard_map/dot_general | solution.py:16
  362.4 7.3 %fusion.22 = f32[256,1024]{1,0:T(8,128)} fusion(bf16[1,3584,1024]{2,1,0:T(8,128)(2,1)} %all-gather.12.cloned.1.call-done, bf16[256,1,3584]{2,1,0:T(2,128)(2,1)} %get-tuple-element.53), kind=kOutput, calls=%fused_computation.27 | convolution fusion | flops 1879048192 | bytes 10223616 | tf_op jit(solution)/shard_map/dot_general | solution.py:17
  369.6 6.4 %fusion.16 = f32[256,1024]{1,0:T(8,128)S(1)} fusion(bf16[1,1024,3584]{2,1,0:T(8,128)(2,1)} %all-gather.14.cloned.1.call-done, bf16[256,1,3584]{2,1,0:T(2,128)(2,1)} %get-tuple-element.54), kind=kOutput, calls=%fused_computation.21 | convolution fusion | flops 1879048192 | bytes 10223616 | tf_op jit(solution)/shard_map/dot_general | solution.py:21
  376.1 1.0 copy-done.11
  377.1 2.2 fusion.20
  379.3 3.9 fusion.34
  383.2 3.7 stack.13
  386.9 5.5 %fusion.31 = bf16[256,3584]{1,0:T(8,128)(2,1)S(1)} fusion(bf16[1,1024,3584]{2,1,0:T(8,128)(2,1)} %all-gather.14.cloned.1.call-done, f32[256,1024]{1,0:T(8,128)} %fusion.22, f32[256,1024]{1,0:T(8,128)S(1)} %fusion.26), kind=kOutput, calls=%fused_computation.34 | convolution fusion | flops 1881538560 | bytes 11272192 | tf_op jit(solution)/shard_map/dot_general | solution.py:20
  392.4 3.8 stack.12
  396.2 9.8 %pad_maximum_fusion = bf16[128,2,2,3584]{3,2,1,0:T(2,128)(2,1)} fusion(bf16[128,2,1,3584]{3,2,1,0:T(2,128)(2,1)} %stack.13, bf16[128,2,1,3584]{3,2,1,0:T(2,128)(2,1)} %stack.12), kind=kLoop, calls=%fused_computation.37 | loop fusion | flops 7340032 | bytes 7340032 | tf_op jit(solution)/shard_map/stack | solution.py:151
  406.0 7.8 %all-to-all-start.2 = ((bf16[128,2,2,3584]{3,2,1,0:T(2,128)(2,1)}), bf16[128,2,2,3584]{3,2,1,0:T(2,128)(2,1)}, u32[]{:S(2)}, u32[]{:S(2)}) async-start(bf16[128,2,2,3584]{3,2,1,0:T(2,128)(2,1)} %pad_maximum_fusion), calls=%async_computation.3 | async-start | bytes 7340032 | tf_op jit(solution)/shard_map/all_to_all | solution.py:152
  413.9 81.0 %all-to-all-done.2 = bf16[128,2,2,3584]{3,2,1,0:T(2,128)(2,1)} async-done(((bf16[128,2,2,3584]{3,2,1,0:T(2,128)(2,1)}), bf16[128,2,2,3584]{3,2,1,0:T(2,128)(2,1)}, u32[]{:S(2)}, u32[]{:S(2)}) %all-to-all-start.2) | async-done | bytes 3670048 | tf_op jit(solution)/shard_map/all_to_all | solution.py:152
  494.9 4.4 copy.63
  499.3 5.9 %copy.50 = bf16[7168,256]{1,0:T(8,128)(2,1)} copy(bf16[7168,256]{0,1:T(8,128)(2,1)} %bitcast.138) | data formatting | bytes 7340032 | tf_op jit(solution)/shard_map/dot_general | solution.py:153
  505.2 3.4 fusion.55
  508.6 1.8 copy-done
  510.3 1.9 fusion.41
  512.3 0.1 copy.57
  512.4 0.1 copy.53
  512.5 3.1 fusion.42
  515.6 3.1 fusion.40
  518.7 0.2 multiply_reduce_fusion
  518.9 0.6 fusion.65
  519.5 0.8 fusion.59
  (45 shorter events, 0.3 us)
Async XLA Ops:
  13.6 8.8 %copy-start.6 = (bf16[1,128,64]{1,2,0:T(8,128)(2,1)S(1)}, bf16[1,128,64]{1,2,0:T(8,128)(2,1)}, u32[]{:S(2)}) copy-start(bf16[1,128,64]{1,2,0:T(8,128)(2,1)} %param.19) | copy-start | bytes 49156
  13.6 138.5 %copy-start.5 = (bf16[1,128,512]{2,1,0:T(8,128)(2,1)S(1)}, bf16[1,128,512]{2,1,0:T(8,128)(2,1)}, u32[]{:S(2)}) copy-start(bf16[1,128,512]{2,1,0:T(8,128)(2,1)} %param.17) | copy-start | bytes 393220
  13.6 180.2 %all-to-all-start = ((bf16[16,8,128,224]{2,1,3,0:T(8,128)(2,1)}), bf16[16,8,128,224]{2,1,3,0:T(8,128)(2,1)}, u32[]{:S(2)}, u32[]{:S(2)}) async-start(bf16[16,8,128,224]{2,1,3,0:T(8,128)(2,1)} %stack.8), calls=%async_computation | async-start | bytes 14680064 | tf_op jit(solution)/shard_map/all_to_all | solution.py:109
  20.8 131.3 %all-gather.6.cloned.1.call-start = ((), (), s32[]{:S(2)}) async-start(), calls=%async_computation.4 | async-start | bytes 2228224 | tf_op jit(solution)/shard_map/all_gather | solution.py:74
  21.5 170.3 %all-gather.8.cloned.1.call-start = ((), (), s32[]{:S(2)}) async-start(), calls=%async_computation.5 | async-start | bytes 1114112 | tf_op jit(solution)/shard_map/all_gather | solution.py:107
  22.3 215.2 %reduce-scatter.2.cloned.1.call-start = ((), (), s32[]{:S(2)}) async-start(), calls=%async_computation.6 | async-start | bytes 1032192 | tf_op jit(solution)/shard_map/reduce_scatter | solution.py:114
  160.5 5.2 copy-start.10
  200.4 12.3 %copy-start.7 = (s32[1,16,8]{1,2,0:T(8,128)S(1)}, s32[1,16,8]{1,2,0:T(8,128)}, u32[]{:S(2)}) copy-start(s32[1,16,8]{1,2,0:T(8,128)} %param.27) | copy-start | bytes 1540
  200.4 37.1 %copy-start.1 = (bf16[1,16,3584]{2,1,0:T(8,128)(2,1)S(1)}, bf16[1,16,3584]{2,1,0:T(8,128)(2,1)}, u32[]{:S(2)}) copy-start(bf16[1,16,3584]{2,1,0:T(8,128)(2,1)} %param.22) | copy-start | bytes 344068
  200.4 38.1 %copy-start.4 = (f32[3584]{0:T(1024)S(1)}, f32[3584]{0:T(1024)}, u32[]{:S(2)}) copy-start(f32[3584]{0:T(1024)} %param.23) | copy-start | bytes 43012
  200.4 39.1 %copy-start.3 = (bf16[1,16,3584]{2,1,0:T(8,128)(2,1)S(1)}, bf16[1,16,3584]{2,1,0:T(8,128)(2,1)}, u32[]{:S(2)}) copy-start(bf16[1,16,3584]{2,1,0:T(8,128)(2,1)} %param.29) | copy-start | bytes 344068
  200.4 155.7 %all-gather.10.cloned.1.call-start = ((), (), s32[]{:S(2)}) async-start(), calls=%async_computation.7 | async-start | bytes 11010048 | tf_op jit(solution)/shard_map/all_gather | solution.py:139
  201.0 161.4 %all-gather.12.cloned.1.call-start = ((), (), s32[]{:S(2)}) async-start(), calls=%async_computation.8 | async-start | bytes 11010048 | tf_op jit(solution)/shard_map/all_gather | solution.py:140
  252.0 95.1 %all-to-all-start.1 = ((bf16[128,2,2,3584]{3,2,1,0:T(2,128)(2,1)}), bf16[128,2,2,3584]{3,2,1,0:T(2,128)(2,1)}, u32[]{:S(2)}, u32[]{:S(2)}) async-start(bf16[128,2,2,3584]{3,2,1,0:T(2,128)(2,1)} %reshape.132), calls=%async_computation.2 | async-start | bytes 7340032 | tf_op jit(solution)/shard_map/all_to_all | solution.py:146
  264.1 105.6 %all-gather.14.cloned.1.call-start = ((), (), s32[]{:S(2)}) async-start(), calls=%async_computation.9 | async-start | bytes 11010048 | tf_op jit(solution)/shard_map/all_gather | solution.py:141
  369.6 7.4 %copy-start.9 = (bf16[1,3584,1024]{2,1,0:T(8,128)(2,1)S(1)}, bf16[1,3584,1024]{2,1,0:T(8,128)(2,1)}, u32[]{:S(2)}) copy-start(bf16[1,3584,1024]{2,1,0:T(8,128)(2,1)} %all-gather.12.cloned.1.call-done) | copy-start | bytes 22020100
  369.6 9.6 %slice-start = ((s8[7340032]{0:T(1024)(128)(4,1)}), s8[4194304]{0:T(1024)(128)(4,1)S(1)}, s32[]{:S(2)}) async-start(s8[7340032]{0:T(1024)(128)(4,1)} %bitcast.145), calls=%async_computation.10 | async-start | bytes 8388608
  376.1 1.0 copy-start.11
  377.1 2.2 slice-start.1
  406.0 7.8 %copy-start.8 = (f32[1,16,8]{1,2,0:T(8,128)S(1)}, f32[1,16,8]{1,2,0:T(8,128)}, u32[]{:S(2)}) copy-start(f32[1,16,8]{1,2,0:T(8,128)} %param.28) | copy-start | bytes 1540
  406.0 88.8 %all-to-all-start.2 = ((bf16[128,2,2,3584]{3,2,1,0:T(2,128)(2,1)}), bf16[128,2,2,3584]{3,2,1,0:T(2,128)(2,1)}, u32[]{:S(2)}, u32[]{:S(2)}) async-start(bf16[128,2,2,3584]{3,2,1,0:T(2,128)(2,1)} %pad_maximum_fusion), calls=%async_computation.3 | async-start | bytes 7340032 | tf_op jit(solution)/shard_map/all_to_all | solution.py:152
  508.6 1.8 copy-start
  508.6 10.1 %copy-start.2 = (bf16[16,3584]{1,0:T(8,128)(2,1)S(1)}, bf16[16,3584]{1,0:T(8,128)(2,1)}, u32[]{:S(2)}) copy-start(bf16[16,3584]{1,0:T(8,128)(2,1)} %reduce-scatter.2.cloned.1.call-done) | copy-start | bytes 344068
Sparse Core Ops, SparseCore 0:
  24.1 117.8 all-gather.5
  144.4 47.4 all-gather.7
  200.5 36.9 reduce-scatter.1
Sparse Core Ops, SparseCore 1:
  202.8 23.0 all-gather.9
  227.6 24.8 all-gather.11
  266.5 24.9 all-gather.13
